TPU v7x, 32 devices: a whole 2x2x4 slice. The times are simulated.
32 devices in a mesh: img: 4 (over y, x), tpl: 8 (over z, core).
Axes of the slice: x: 2, y: 2, z: 4, core: 2. Of those that a mesh axis runs over, the one named last changes fastest.
Arguments:
- images: bfloat16 [6144, 2048], P(('img', 'tpl')), may hold values from -320 to 320
- templates: bfloat16 [3072, 2048], P('tpl'), may hold values from -0.62 to 0.62
- class_exponent: int32 [8], replicated, may hold values from 0 to 5
- class_mask: int32 [6144, 8], P('img'), may hold values from 0 to 1, as said below
Outputs:
- new_templates: float32 [3072, 2048], P('tpl', 'img')
- log_evidence: float32 [6144], P('img')
Inputs may be any that keep to these rules, and one draw needn't show every extreme that they name: `class_mask`: every image is compared with at least one class.
All inputs are finite; a program needn't handle non-finite values.
Results may differ from a plain program's by a relative error of at most 0.0023.
Values may be sent and summed in bfloat16 or wider, within the bound.
A program may use at most 64 MiB of HBM per device.

v0:
```python
import jax
import jax.numpy as jnp
from jax import lax
from jax.sharding import PartitionSpec as P

floor_score = -1e30


def per_device(images, templates, class_exponent, class_mask):
    tpl_rows = templates.shape[0]
    feature_count = templates.shape[1]
    class_count = class_exponent.shape[0]
    per_class = tpl_rows * lax.axis_size("tpl") // class_count
    global_rows = lax.axis_index("tpl") * tpl_rows + jnp.arange(tpl_rows, dtype=jnp.int32)
    owner = global_rows // per_class
    onehot = (jnp.arange(class_count, dtype=jnp.int32)[:, None] == owner[None, :]).astype(
        jnp.float32
    )
    inverse_temp = 0.5 * jnp.exp2(0.5 * class_exponent.astype(jnp.float32))
    template_beta = jnp.sum(onehot * inverse_temp[:, None], axis=0)
    allowed = jnp.dot(class_mask.astype(jnp.float32), onehot, precision=lax.Precision.HIGHEST) > 0.5
    squared_norm = jnp.sum(jnp.square(templates.astype(jnp.float32)), axis=1)
    gathered = lax.all_gather(images, "tpl", axis=0, tiled=True)
    raw = lax.dot_general(
        gathered, templates, (((1,), (1,)), ((), ())), preferred_element_type=jnp.float32
    )
    scores = template_beta[None, :] * (raw - 0.5 * squared_norm[None, :])
    local_top = jnp.max(jnp.where(allowed, scores, floor_score), axis=1)
    top = lax.pmax(local_top, "tpl")
    expo = jnp.where(allowed, jnp.exp(scores - top[:, None]), 0.0)
    totals = lax.psum(jnp.sum(expo, axis=1), "tpl")
    posterior = expo / totals[:, None]
    posterior_bf = posterior.astype(jnp.bfloat16)
    occupancy_part = jnp.sum(posterior, axis=0)
    weighted_part = lax.dot_general(
        posterior_bf, gathered, (((0,), (0,)), ((), ())), preferred_element_type=jnp.float32
    )
    columns = feature_count // lax.axis_size("img")
    col_start = lax.axis_index("img") * columns
    own_share = lax.psum_scatter(weighted_part, "img", scatter_dimension=1, tiled=True)
    occupancy = lax.psum(occupancy_part, "img")
    own_templates = lax.dynamic_slice_in_dim(templates, col_start, columns, 1).astype(jnp.float32)
    new_templates = (own_share + own_templates) / (occupancy[:, None] + 1.0)
    log_evidence = top + jnp.log(totals)
    return (new_templates, log_evidence)


def solution(mesh):
    in_specs = (P(("img", "tpl"), None), P("tpl", None), P(), P("img", None))
    out_specs = (P("tpl", "img"), P("img"))
    return jax.shard_map(
        per_device, mesh=mesh, in_specs=in_specs, out_specs=out_specs, check_vma=False
    )
```

profile of v0, /device:TPU:0, one launch (start us, length us, event | category | flops | bytes accessed | tf_op | source)
XLA Modules:
  0.0 171.4 jit_solution(5243481778394577077)
XLA Ops:
  7.2 0.0 all-gather.2.cloned.1.call-start
  7.2 0.7 all-gather.2.cloned.1.call-update
  7.9 0.0 reduce-scatter.2.cloned.1.call-start
  8.0 0.7 exponential_multiply_fusion
  8.6 0.1 select_reduce_fusion.1
  8.7 1.8 %multiply_reduce_fusion = f32[384]{0:T(512)S(1)} fusion(bf16[384,2048]{1,0:T(8,128)(2,1)} %param.5), kind=kLoop, calls=%fused_computation | loop fusion | flops 2358912 | bytes 1574400 | tf_op jit(solution)/shard_map/reduce_sum | solution.py:22
  10.5 0.0 copy-start
  10.5 66.5 %all-gather.2.cloned.1.call-done = bf16[1536,2048]{1,0:T(8,128)(2,1)} async-done(((bf16[192,2048]{1,0:T(8,128)(2,1)}), bf16[1536,2048]{1,0:T(8,128)(2,1)}) %all-gather.2.cloned.1.call-update) | async-done | bytes 6291472 | tf_op jit(solution)/shard_map/all_gather | solution.py:23
  77.1 5.2 %fusion = f32[1536,384]{0,1:T(8,128)S(1)} fusion(bf16[1536,2048]{1,0:T(8,128)(2,1)} %all-gather.2.cloned.1.call-done, bf16[384,2048]{1,0:T(8,128)(2,1)} %param.5, f32[384]{0:T(512)S(1)} %broadcast_multiply_fusion, f32[384]{0:T(512)S(1)} %select_reduce_fusion.1), kind=kOutput, calls=%fused_computation.2 | convolution fusion | flops 2417098752 | bytes 10226688 | tf_op jit(solution)/shard_map/dot_general | solution.py:24
  82.3 0.0 copy-done
  82.3 1.5 select_reduce_fusion
  83.8 14.4 %pmax.7 = f32[1536]{0:T(1024)S(1)} all-reduce(f32[1536]{0:T(1024)S(1)} %get-tuple-element.2), channel_id=1, replica_groups=mesh['img'=4,'tpl'=8] {'tpl'}, use_global_device_ids=true, to_apply=%region_3.4 | all-reduce | flops 1536 | bytes 12288 | tf_op jit(solution)/shard_map/pmax | solution.py:29
  98.3 0.6 fusion.3
  98.8 13.9 %psum.14 = f32[1536]{0:T(1024)S(1)} all-reduce(f32[1536]{0:T(1024)S(1)} %fusion.3), channel_id=1, replica_groups=mesh['img'=4,'tpl'=8] {'tpl'}, use_global_device_ids=true, to_apply=%region_5.6 | all-reduce | flops 1536 | bytes 12288 | tf_op jit(solution)/shard_map/psum | solution.py:31
  112.8 7.1 %fusion.4 = f32[384,2048]{1,0:T(8,128)} fusion(bf16[1536,2048]{1,0:T(8,128)(2,1)} %all-gather.2.cloned.1.call-done, pred[1536,384]{0,1:T(32,128)(4,1)S(1)} %get-tuple-element.3, f32[1536,384]{0,1:T(8,128)S(1)} %fusion, f32[1536]{0:T(1024)S(1)} %psum.14, f32[1536]{0:T(1024)S(1)} %pmax.7), kind=kOutput, calls=%fused_computation.9 | convolution fusion | flops 2418278400 | bytes 12398592 | tf_op jit(solution)/shard_map/dot_general | solution.py:35
  119.9 0.0 reduce-scatter.2.cloned.1.call-update
  119.9 0.7 fusion.6
  120.6 10.4 %psum.15 = f32[384]{0:T(512)S(1)} all-reduce(f32[384]{0:T(512)S(1)} %fusion.6), channel_id=1, replica_groups=mesh['img'=4,'tpl'=8] {'img'}, use_global_device_ids=true, to_apply=%region_8.9 | all-reduce | flops 384 | bytes 3072 | tf_op jit(solution)/shard_map/psum | solution.py:41
  131.0 0.6 log_add_fusion
  131.6 30.7 %reduce-scatter.2.cloned.1.call-done = f32[384,512]{1,0:T(8,128)} async-done(((f32[384,2048]{1,0:T(8,128)}), f32[384,512]{1,0:T(8,128)}) %reduce-scatter.2.cloned.1.call-update) | async-done | bytes 786448 | tf_op jit(solution)/shard_map/reduce_scatter | solution.py:40
  162.3 2.2 %add_divide_fusion = f32[384,512]{1,0:T(8,128)} fusion(f32[384,512]{1,0:T(8,128)} %reduce-scatter.2.cloned.1.call-done, f32[384]{0:T(512)S(1)} %broadcast_add_fusion, bf16[384,2048]{1,0:T(8,128)(2,1)} %param.5, s32[]{:T(128)S(6)} %select_n.22), kind=kLoop, calls=%fused_computation.11 | loop fusion | flops 589824 | bytes 1967620 | tf_op jit(solution)/shard_map/div | solution.py:43
  (3 shorter events, 0.0 us)
Async XLA Ops:
  7.2 69.9 %all-gather.2.cloned.1.call-start = ((), (), s32[]{:S(2)}) async-start(), calls=%async_computation.1 | async-start | bytes 7077888 | tf_op jit(solution)/shard_map/all_gather | solution.py:23
  7.9 154.4 %reduce-scatter.2.cloned.1.call-start = ((), (), s32[]{:S(2)}) async-start(), calls=%async_computation.2 | async-start | bytes 3932160 | tf_op jit(solution)/shard_map/reduce_scatter | solution.py:40
  10.5 71.8 %copy-start = (s32[1536,8]{0,1:T(8,128)S(1)}, s32[1536,8]{0,1:T(8,128)}, u32[]{:S(2)}) copy-start(s32[1536,8]{0,1:T(8,128)} %param.7) | copy-start | bytes 147460
Sparse Core Ops, SparseCore 0:
  9.6 67.4 all-gather.1
  120.0 42.2 reduce-scatter.1
where the time goes:
time: 172 us; the launch traced here: 171 us
  waiting for transfers between devices  97.9 us (57%)
  blocking collectives  38.7 us (23%)
  between operations  14.1 us (8%)
  matrix products  13.9 us (8%)
  other arithmetic  6.69 us (4%)
    all_gather x1, waiting for transfers between devices, per_device(): gathered = lax.all_gather(images, 'tpl', axis=0, tiled=True)  66.5 us
    reduce_scatter x1, waiting for transfers between devices, per_device(): lax.psum_scatter(weighted_part, 'img', scatter_dimension=1, tiled=True)  30.7 us
    pmax x1, blocking collectives, per_device(): top = lax.pmax(local_top, 'tpl')  14.4 us
    psum x1, blocking collectives, per_device(): totals = lax.psum(jnp.sum(expo, axis=1), 'tpl')  13.9 us
    psum x1, blocking collectives, per_device(): occupancy = lax.psum(occupancy_part, 'img')  10.4 us
    dot_general x1, matrix products, per_device(): lax.dot_general(posterior_bf, gathered, (((0,), (0,)), ((), ())), preferr...  7.11 us
    dot_general x1, matrix products, per_device(): lax.dot_general(gathered, templates, (((1,), (1,)), ((), ())), preferred_...  5.24 us
  transfers between devices with their start and end apart: 2, of which 2 were waited for; matrix products, arithmetic and copies ran while one was open for 2% of the time, Pallas kernels for 0%

commit v1 on v0

--- a/solution.py
+++ b/solution.py
@@ -20,7 +20,12 @@
     template_beta = jnp.sum(onehot * inverse_temp[:, None], axis=0)
     allowed = jnp.dot(class_mask.astype(jnp.float32), onehot, precision=lax.Precision.HIGHEST) > 0.5
     squared_norm = jnp.sum(jnp.square(templates.astype(jnp.float32)), axis=1)
-    gathered = lax.all_gather(images, "tpl", axis=0, tiled=True)
+    ring = [images]
+    for hop in range(7):
+        ring.append(lax.ppermute(ring[-1], "tpl", [(dev, (dev + 1) % 8) for dev in range(8)]))
+    gathered = jnp.roll(
+        jnp.concatenate(ring[::-1], axis=0), (lax.axis_index("tpl") + 1) * ring[0].shape[0], axis=0
+    )
     raw = lax.dot_general(
         gathered, templates, (((1,), (1,)), ((), ())), preferred_element_type=jnp.float32
     )

time: 172 us -> 205 us (1.19)
  waiting for transfers between devices: 97.9 us -> 122 us
  local copies, waits for them, and re-layouts: 0.01 us -> 10.4 us
  matrix products: 13.9 us -> 11.7 us
    ppermute x0 -> x7, waiting for transfers between devices: none -> 91.6 us  [per_device(): lax.ppermute(ring[-1], 'tpl', [(dev, (dev + 1) % 8) for dev in range(8)])]
    all_gather x1 -> x0, waiting for transfers between devices: 66.5 us -> none  [per_device(): gathered = lax.all_gather(images, 'tpl', axis=0, tiled=True)]
    unnamed x2 -> x23, local copies, waits for them, and re-layouts: 0.01 us -> 10.4 us
    dot_general x1, matrix products: 5.24 us -> 2.66 us  [per_device(): lax.dot_general(gathered, templates, (((1,), (1,)), ((), ())), preferred_...]
  transfers between devices with their start and end apart: 2 -> 8, of which waited for: 2 -> 8; matrix products, arithmetic and copies ran while one was open for 2% -> 2% of each run, Pallas kernels for 0% -> 0%
where the time goes in v1:
time: 205 us
  waiting for transfers between devices  122 us (60%)
  blocking collectives  38.5 us (19%)
  between operations  14.3 us (7%)
  matrix products  11.7 us (6%)
  local copies, waits for them, and re-layouts  10.4 us (5%)
  other arithmetic  6.67 us (3%)
    ppermute x7, waiting for transfers between devices, per_device(): lax.ppermute(ring[-1], 'tpl', [(dev, (dev + 1) % 8) for dev in range(8)])  91.6 us
    reduce_scatter x1, waiting for transfers between devices, per_device(): lax.psum_scatter(weighted_part, 'img', scatter_dimension=1, tiled=True)  30.7 us
    psum x1, blocking collectives, per_device(): totals = lax.psum(jnp.sum(expo, axis=1), 'tpl')  13.9 us
    pmax x1, blocking collectives, per_device(): top = lax.pmax(local_top, 'tpl')  13.9 us
    psum x1, blocking collectives, per_device(): occupancy = lax.psum(occupancy_part, 'img')  10.7 us
    unnamed x23, local copies, waits for them, and re-layouts  10.4 us
    dot_general x1, matrix products, per_device(): lax.dot_general(posterior_bf, gathered, (((0,), (0,)), ((), ())), preferr...  7.47 us
  transfers between devices with their start and end apart: 8, of which 8 were waited for; matrix products, arithmetic and copies ran while one was open for 2% of the time, Pallas kernels for 0%

profile of v1, /device:TPU:0, one launch (start us, length us, event | category | flops | bytes accessed | tf_op | source)
XLA Modules:
  0.0 204.5 jit_solution(11704750248180981720)
XLA Ops:
  7.2 0.5 collective-permute-start
  7.8 13.9 %collective-permute-done = bf16[192,2048]{1,0:T(8,128)(2,1)S(1)} collective-permute-done((bf16[192,2048]{1,0:T(8,128)(2,1)}, bf16[192,2048]{1,0:T(8,128)(2,1)S(1)}, u32[]{:S(2)}, u32[]{:S(2)}) %collective-permute-start) | collective-permute-done | bytes 786464 | tf_op jit(solution)/shard_map/ppermute | solution.py:25
  21.7 13.2 %collective-permute-done.1 = bf16[192,2048]{1,0:T(8,128)(2,1)S(1)} collective-permute-done((bf16[192,2048]{1,0:T(8,128)(2,1)S(1)}, bf16[192,2048]{1,0:T(8,128)(2,1)S(1)}, u32[]{:S(2)}, u32[]{:S(2)}) %collective-permute-start.1) | collective-permute-done | bytes 786464 | tf_op jit(solution)/shard_map/ppermute | solution.py:25
  34.9 13.2 %collective-permute-done.2 = bf16[192,2048]{1,0:T(8,128)(2,1)S(1)} collective-permute-done((bf16[192,2048]{1,0:T(8,128)(2,1)S(1)}, bf16[192,2048]{1,0:T(8,128)(2,1)S(1)}, u32[]{:S(2)}, u32[]{:S(2)}) %collective-permute-start.2) | collective-permute-done | bytes 786464 | tf_op jit(solution)/shard_map/ppermute | solution.py:25
  48.1 13.3 %collective-permute-done.3 = bf16[192,2048]{1,0:T(8,128)(2,1)} collective-permute-done((bf16[192,2048]{1,0:T(8,128)(2,1)S(1)}, bf16[192,2048]{1,0:T(8,128)(2,1)}, u32[]{:S(2)}, u32[]{:S(2)}) %collective-permute-start.3) | collective-permute-done | bytes 786464 | tf_op jit(solution)/shard_map/ppermute | solution.py:25
  61.4 13.5 %collective-permute-done.4 = bf16[192,2048]{1,0:T(8,128)(2,1)} collective-permute-done((bf16[192,2048]{1,0:T(8,128)(2,1)}, bf16[192,2048]{1,0:T(8,128)(2,1)}, u32[]{:S(2)}, u32[]{:S(2)}) %collective-permute-start.4) | collective-permute-done | bytes 786464 | tf_op jit(solution)/shard_map/ppermute | solution.py:25
  75.0 13.5 %collective-permute-done.5 = bf16[192,2048]{1,0:T(8,128)(2,1)} collective-permute-done((bf16[192,2048]{1,0:T(8,128)(2,1)}, bf16[192,2048]{1,0:T(8,128)(2,1)}, u32[]{:S(2)}, u32[]{:S(2)}) %collective-permute-start.5) | collective-permute-done | bytes 786464 | tf_op jit(solution)/shard_map/ppermute | solution.py:25
  88.5 0.7 exponential_multiply_fusion
  89.2 0.1 select_reduce_fusion.1
  89.3 1.8 multiply_reduce_fusion
  91.1 10.9 %collective-permute-done.6 = bf16[192,2048]{1,0:T(8,128)(2,1)} collective-permute-done((bf16[192,2048]{1,0:T(8,128)(2,1)}, bf16[192,2048]{1,0:T(8,128)(2,1)}, u32[]{:S(2)}, u32[]{:S(2)}) %collective-permute-start.6) | collective-permute-done | bytes 786464 | tf_op jit(solution)/shard_map/ppermute | solution.py:25
  102.0 1.2 constant_dynamic-update-slice_fusion.15
  103.2 1.2 constant_dynamic-update-slice_fusion.14
  104.4 1.2 constant_dynamic-update-slice_fusion.13
  105.6 1.2 constant_dynamic-update-slice_fusion.12
  106.8 0.1 constant_dynamic-update-slice_fusion.11
  107.1 1.2 constant_dynamic-update-slice_fusion.7
  108.3 1.2 constant_dynamic-update-slice_fusion.6
  109.5 1.2 constant_dynamic-update-slice_fusion.5
  110.7 1.2 constant_dynamic-update-slice_fusion.4
  112.2 2.7 %fusion.7 = f32[1536,384]{0,1:T(8,128)S(1)} fusion(bf16[384,2048]{1,0:T(8,128)(2,1)S(1)} %copy-done.1, bf16[3072,2048]{1,0:T(8,128)(2,1)S(1)} %constant_dynamic-update-slice_fusion, s32[]{:T(128)S(6)} %select_n.34, f32[384]{0:T(512)S(1)} %broadcast_multiply_fusion, f32[384]{0:T(512)S(1)} %select_reduce_fusion.1), kind=kOutput, calls=%fused_computation.6 | convolution fusion | flops 2417098752 | bytes 10227716 | tf_op jit(solution)/shard_map/dot_general | solution.py:29
  114.9 1.5 select_reduce_fusion
  116.4 0.4 copy-done.2
  116.8 13.9 %pmax.7 = f32[1536]{0:T(1024)S(1)} all-reduce(f32[1536]{0:T(1024)S(1)} %get-tuple-element.2), channel_id=1, replica_groups=mesh['img'=4,'tpl'=8] {'tpl'}, use_global_device_ids=true, to_apply=%region_3.4 | all-reduce | flops 1536 | bytes 12288 | tf_op jit(solution)/shard_map/pmax | solution.py:34
  130.7 0.6 fusion.12
  131.2 13.9 %psum.14 = f32[1536]{0:T(1024)S(1)} all-reduce(f32[1536]{0:T(1024)S(1)} %fusion.12), channel_id=1, replica_groups=mesh['img'=4,'tpl'=8] {'tpl'}, use_global_device_ids=true, to_apply=%region_5.6 | all-reduce | flops 1536 | bytes 12288 | tf_op jit(solution)/shard_map/psum | solution.py:36
  145.2 7.5 %fusion = f32[384,2048]{1,0:T(8,128)} fusion(bf16[3072,2048]{1,0:T(8,128)(2,1)} %copy-done.2, s32[]{:T(128)S(6)} %select_n.34, pred[1536,384]{0,1:T(32,128)(4,1)S(1)} %get-tuple-element.3, f32[1536,384]{0,1:T(8,128)S(1)} %fusion.7, f32[1536]{0:T(1024)S(1)} %psum.14, f32[1536]{0:T(1024)S(1)} %pmax.7), kind=kOutput, calls=%fused_computation | convolution fusion | flops 2418278400 | bytes 12398596 | tf_op jit(solution)/shard_map/dot_general | solution.py:40
  152.7 0.7 fusion.14
  153.4 10.7 %psum.15 = f32[384]{0:T(512)S(1)} all-reduce(f32[384]{0:T(512)S(1)} %fusion.14), channel_id=1, replica_groups=mesh['img'=4,'tpl'=8] {'img'}, use_global_device_ids=true, to_apply=%region_8.9 | all-reduce | flops 384 | bytes 3072 | tf_op jit(solution)/shard_map/psum | solution.py:46
  164.1 0.6 log_add_fusion
  164.7 30.7 %reduce-scatter.2.cloned.1.call-done = f32[384,512]{1,0:T(8,128)} async-done(((f32[384,2048]{1,0:T(8,128)}), f32[384,512]{1,0:T(8,128)}) %reduce-scatter.2.cloned.1.call-update) | async-done | bytes 786448 | tf_op jit(solution)/shard_map/reduce_scatter | solution.py:45
  195.4 2.2 %add_divide_fusion = f32[384,512]{1,0:T(8,128)} fusion(f32[384,512]{1,0:T(8,128)} %reduce-scatter.2.cloned.1.call-done, f32[384]{0:T(512)S(1)} %broadcast_add_fusion, bf16[384,2048]{1,0:T(8,128)(2,1)} %param.5, s32[]{:T(128)S(6)} %select_n.37), kind=kLoop, calls=%fused_computation.14 | loop fusion | flops 589824 | bytes 1967620 | tf_op jit(solution)/shard_map/div | solution.py:48
  (25 shorter events, 0.5 us)
Async XLA Ops:
  7.2 99.9 %copy-start = (bf16[192,2048]{1,0:T(8,128)(2,1)S(1)}, bf16[192,2048]{1,0:T(8,128)(2,1)}, u32[]{:S(2)}) copy-start(bf16[192,2048]{1,0:T(8,128)(2,1)} %param.4) | copy-start | bytes 2359300
  7.2 188.3 %reduce-scatter.2.cloned.1.call-start = ((), (), s32[]{:S(2)}) async-start(), calls=%async_computation.1 | async-start | bytes 3932160 | tf_op jit(solution)/shard_map/reduce_scatter | solution.py:45
  7.2 14.5 %collective-permute-start = (bf16[192,2048]{1,0:T(8,128)(2,1)}, bf16[192,2048]{1,0:T(8,128)(2,1)S(1)}, u32[]{:S(2)}, u32[]{:S(2)}) collective-permute-start(bf16[192,2048]{1,0:T(8,128)(2,1)} %param.4), channel_id=1, source_target_pairs={{0,1},{1,2},{2,3},{3,4},{4,5},{5,6},{6,7},{7,0},{8,9},{9,10},{10,1... | collective-permute-start | bytes 2359304 | tf_op jit(solution)/shard_map/ppermute | solution.py:25
  21.7 13.2 %collective-permute-start.1 = (bf16[192,2048]{1,0:T(8,128)(2,1)S(1)}, bf16[192,2048]{1,0:T(8,128)(2,1)S(1)}, u32[]{:S(2)}, u32[]{:S(2)}) collective-permute-start(bf16[192,2048]{1,0:T(8,128)(2,1)S(1)} %collective-permute-done), channel_id=1, source_target_pairs={{0,1},{1,2},{2,3},{3,4},{4,5},{5,6},{6,7},{7,0},{8,9},{9,10},{10,1... | collective-permute-start | bytes 2359304 | tf_op jit(solution)/shard_map/ppermute | solution.py:25
  34.9 13.2 %collective-permute-start.2 = (bf16[192,2048]{1,0:T(8,128)(2,1)S(1)}, bf16[192,2048]{1,0:T(8,128)(2,1)S(1)}, u32[]{:S(2)}, u32[]{:S(2)}) collective-permute-start(bf16[192,2048]{1,0:T(8,128)(2,1)S(1)} %collective-permute-done.1), channel_id=1, source_target_pairs={{0,1},{1,2},{2,3},{3,4},{4,5},{5,6},{6,7},{7,0},{8,9},{9,10},{10,1... | collective-permute-start | bytes 2359304 | tf_op jit(solution)/shard_map/ppermute | solution.py:25
  48.1 13.3 %collective-permute-start.3 = (bf16[192,2048]{1,0:T(8,128)(2,1)S(1)}, bf16[192,2048]{1,0:T(8,128)(2,1)}, u32[]{:S(2)}, u32[]{:S(2)}) collective-permute-start(bf16[192,2048]{1,0:T(8,128)(2,1)S(1)} %collective-permute-done.2), channel_id=1, source_target_pairs={{0,1},{1,2},{2,3},{3,4},{4,5},{5,6},{6,7},{7,0},{8,9},{9,10},{10,1... | collective-permute-start | bytes 2359304 | tf_op jit(solution)/shard_map/ppermute | solution.py:25
  61.4 13.5 %collective-permute-start.4 = (bf16[192,2048]{1,0:T(8,128)(2,1)}, bf16[192,2048]{1,0:T(8,128)(2,1)}, u32[]{:S(2)}, u32[]{:S(2)}) collective-permute-start(bf16[192,2048]{1,0:T(8,128)(2,1)} %collective-permute-done.3), channel_id=1, source_target_pairs={{0,1},{1,2},{2,3},{3,4},{4,5},{5,6},{6,7},{7,0},{8,9},{9,10},{10,1... | collective-permute-start | bytes 2359304 | tf_op jit(solution)/shard_map/ppermute | solution.py:25
  74.9 13.5 %collective-permute-start.5 = (bf16[192,2048]{1,0:T(8,128)(2,1)}, bf16[192,2048]{1,0:T(8,128)(2,1)}, u32[]{:S(2)}, u32[]{:S(2)}) collective-permute-start(bf16[192,2048]{1,0:T(8,128)(2,1)} %collective-permute-done.4), channel_id=1, source_target_pairs={{0,1},{1,2},{2,3},{3,4},{4,5},{5,6},{6,7},{7,0},{8,9},{9,10},{10,1... | collective-permute-start | bytes 2359304 | tf_op jit(solution)/shard_map/ppermute | solution.py:25
  88.5 13.5 %collective-permute-start.6 = (bf16[192,2048]{1,0:T(8,128)(2,1)}, bf16[192,2048]{1,0:T(8,128)(2,1)}, u32[]{:S(2)}, u32[]{:S(2)}) collective-permute-start(bf16[192,2048]{1,0:T(8,128)(2,1)} %collective-permute-done.5), channel_id=1, source_target_pairs={{0,1},{1,2},{2,3},{3,4},{4,5},{5,6},{6,7},{7,0},{8,9},{9,10},{10,1... | collective-permute-start | bytes 2359304 | tf_op jit(solution)/shard_map/ppermute | solution.py:25
  91.1 21.1 %copy-start.1 = (bf16[384,2048]{1,0:T(8,128)(2,1)S(1)}, bf16[384,2048]{1,0:T(8,128)(2,1)}, u32[]{:S(2)}) copy-start(bf16[384,2048]{1,0:T(8,128)(2,1)} %param.5) | copy-start | bytes 4718596
  110.7 4.2 %copy-start.3 = (s32[1536,8]{0,1:T(8,128)S(1)}, s32[1536,8]{0,1:T(8,128)}, u32[]{:S(2)}) copy-start(s32[1536,8]{0,1:T(8,128)} %param.7) | copy-start | bytes 147460
  112.2 4.6 %copy-start.2 = (bf16[3072,2048]{1,0:T(8,128)(2,1)}, bf16[3072,2048]{1,0:T(8,128)(2,1)S(1)}, u32[]{:S(2)}) copy-start(bf16[3072,2048]{1,0:T(8,128)(2,1)S(1)} %constant_dynamic-update-slice_fusion) | copy-start | bytes 37748740
Sparse Core Ops, SparseCore 0:
  152.8 42.6 reduce-scatter.1
